TPU v7x, 512 devices: a whole 4x8x8 slice. The times are simulated.
512 devices in a mesh: dp: 32 (over z, x_hi, core), fsdp: 16 (over x_lo, y).
Axes of the slice: x: 4 (x_hi: 2, x_lo: 2; x = x_hi * 2 + x_lo), y: 8, z: 8, core: 2. Of those that a mesh axis runs over, the one named last changes fastest.
Arguments:
- tokens: bfloat16 [5120, 4608], P('fsdp'), may hold values from -12 to 12
- cotangent: bfloat16 [5120, 12288], P('fsdp', 'dp'), may hold values from -0.046875 to 0.046875
- gain: float32 [4608], replicated, may hold values from 0.5 to 1.5
- master: float32 [4608, 12288], P('fsdp', 'dp'), may hold values from -0.09375 to 0.09375
- momentum: float32 [4608, 12288], P('fsdp', 'dp'), may hold values from -3 to 3
Outputs:
- new_master: float32 [4608, 12288], P('fsdp', 'dp')
- new_momentum: float32 [4608, 12288], P('fsdp', 'dp')
All inputs are finite; a program needn't handle non-finite values.
Results may differ from a plain program's by a relative error of at most 0.0024.
Values may be sent and summed in bfloat16 or wider, within the bound.
A program may use at most 64 MiB of HBM per device.

v0:
```python
import math
import jax
import jax.numpy as jnp
from jax import lax
from jax.sharding import PartitionSpec as P

FF = 12288
inv_root_two = 1.0 / math.sqrt(2.0)
inv_root_two_pi = 1.0 / math.sqrt(2.0 * math.pi)


def norm_rows(tokens, gain):
    values = tokens.astype(jnp.float32)
    meansq = jnp.mean(values * values, axis=1, keepdims=True)
    return (values * lax.rsqrt(meansq + 1e-06) * gain).astype(jnp.bfloat16)


def slope_of(pre):
    cdf = 0.5 * (1.0 + jax.scipy.special.erf(pre * inv_root_two))
    return cdf + pre * jnp.exp(-0.5 * pre * pre) * inv_root_two_pi


def local(tokens, cotangent, gain, master, momentum):
    own_rows = master.shape[0]
    own_tokens = tokens.shape[0]
    n_shard = lax.axis_size("fsdp")
    n_copy = lax.axis_size("dp")
    share = own_tokens // n_copy
    along_rows = (((0,), (0,)), ((), ()))
    along_features = (((1,), (1,)), ((), ()))
    cot = cotangent.astype(jnp.float32)
    normed = norm_rows(tokens, gain)
    weights = lax.all_gather(master.astype(jnp.bfloat16), "fsdp", axis=0, tiled=True)
    mine = lax.dynamic_slice_in_dim(normed, lax.axis_index("dp") * share, share, 0)
    some = lax.all_gather(mine, "fsdp", axis=0, tiled=True)
    gram = lax.dot_general(some, normed, along_features, preferred_element_type=jnp.float32).astype(
        jnp.bfloat16
    )
    columns = lax.dynamic_slice_in_dim(some, lax.axis_index("fsdp") * own_rows, own_rows, 1)
    both = lax.all_gather(jnp.concatenate([gram, columns], axis=1), "dp", axis=0, tiled=True)
    both = both.reshape(n_copy, n_shard, share, own_tokens + own_rows)
    both = both.transpose(1, 0, 2, 3).reshape(n_shard * own_tokens, own_tokens + own_rows)
    gram_all = both[:, :own_tokens]
    columns_all = both[:, own_tokens:]

    def gathered(pre):
        dpre = (cot * slope_of(pre)).astype(jnp.bfloat16)
        return (dpre, lax.all_gather(dpre, "fsdp", axis=0, tiled=True))

    pre = jnp.dot(normed, weights, preferred_element_type=jnp.float32)
    dpre, dpre_all = gathered(pre)
    shift = lax.dot_general(gram_all, dpre_all, along_rows, preferred_element_type=jnp.float32)
    squares = lax.psum(jnp.sum(dpre.astype(jnp.float32) * shift), ("dp", "fsdp"))
    scale = math.sqrt(FF) / 4.0 / (jnp.sqrt(jnp.maximum(squares, 0.0)) + 1e-12)
    unused, dpre_two = gathered(pre + scale * shift)
    second = lax.dot_general(columns_all, dpre_two, along_rows, preferred_element_type=jnp.float32)
    new_momentum = 0.9 * momentum + second
    new_master = master - 0.002 * new_momentum
    return (new_master, new_momentum)


def solution(mesh):
    in_specs = (P("fsdp", None), P("fsdp", "dp"), P(), P("fsdp", "dp"), P("fsdp", "dp"))
    out_specs = (P("fsdp", "dp"), P("fsdp", "dp"))
    return jax.shard_map(local, mesh=mesh, in_specs=in_specs, out_specs=out_specs, check_vma=False)
```

profile of v0, /device:TPU:4, one launch (start us, length us, event | category | flops | bytes accessed | tf_op | source)
XLA Modules:
  0.0 539.6 jit_solution(4000123411859568000)
XLA Ops:
  7.2 0.0 all-gather.15.cloned.1.call-start
  7.2 0.0 copy-start
  7.2 2.6 fusion
  9.8 2.7 fusion.2
  12.5 0.7 dynamic-slice_bitcast_fusion
  13.2 0.0 all-gather.15.cloned.1.call-update
  13.2 0.0 all-gather.9.cloned.1.call-start
  13.3 0.0 copy-done
  13.3 0.7 convert_element_type.28
  14.0 0.0 all-gather.9.cloned.1.call-update
  14.0 0.0 all-gather.7.cloned.1.call-start
  14.1 77.9 %all-gather.15.cloned.1.call-done = bf16[16,10,4608]{2,1,0:T(8,128)(2,1)} async-done(((bf16[1,10,4608]{2,1,0:T(8,128)(2,1)}), bf16[16,10,4608]{2,1,0:T(8,128)(2,1)}) %all-gather.15.cloned.1.call-update) | async-done | bytes 1474576 | tf_op jit(solution)/shard_map/all_gather | solution.py:35
  92.0 2.8 reshape.22
  94.7 1.0 constant_dynamic-slice_fusion
  95.8 2.6 convolution_convert_fusion
  98.4 0.8 pad_maximum_fusion
  99.2 0.0 all-gather.7.cloned.1.call-update
  99.2 0.0 all-gather.11.cloned.1.call-start
  99.2 70.5 %all-gather.9.cloned.1.call-done = bf16[4608,384]{1,0:T(8,128)(2,1)} async-done(((bf16[288,384]{1,0:T(8,128)(2,1)}), bf16[4608,384]{1,0:T(8,128)(2,1)}) %all-gather.9.cloned.1.call-update) | async-done | bytes 3538960 | tf_op jit(solution)/shard_map/all_gather | solution.py:33
  169.7 4.5 fusion.10
  174.2 0.0 all-gather.11.cloned.1.call-update
  174.3 0.0 all-gather.13.cloned.1.call-start
  174.3 96.1 %all-gather.7.cloned.1.call-done = bf16[5120,608]{1,0:T(8,128)(2,1)} async-done(((bf16[160,608]{1,0:T(8,128)(2,1)}), bf16[5120,608]{1,0:T(8,128)(2,1)}) %all-gather.7.cloned.1.call-update) | async-done | bytes 6225936 | tf_op jit(solution)/shard_map/all_gather | solution.py:40
  270.4 12.8 %reshape.19 = bf16[32,16,10,608]{3,2,1,0:T(8,128)(2,1)} reshape(bf16[5120,608]{1,0:T(8,128)(2,1)} %all-gather.7.cloned.1.call-done) | data formatting | bytes 12451840 | tf_op jit(solution)/shard_map/reshape | solution.py:41
  283.2 9.3 %copy.8 = bf16[16,32,10,608]{3,2,1,0:T(8,128)(2,1)} copy(bf16[16,32,10,608]{3,2,0,1:T(8,128)(2,1)} %bitcast.9) | data formatting | bytes 12451840 | tf_op jit(solution)/shard_map/transpose | solution.py:42
  292.4 0.0 copy-start.3
  292.4 13.6 %reshape.20 = bf16[5120,608]{1,0:T(8,128)(2,1)} reshape(bf16[16,32,10,608]{3,2,1,0:T(8,128)(2,1)} %copy.8) | data formatting | bytes 12451840 | tf_op jit(solution)/shard_map/reshape | solution.py:42
  306.1 0.0 copy-start.2
  306.1 0.0 copy-start.1
  306.1 0.0 copy-start.4
  306.1 43.4 %all-gather.11.cloned.1.call-done = bf16[5120,384]{1,0:T(8,128)(2,1)} async-done(((bf16[320,384]{1,0:T(8,128)(2,1)}), bf16[5120,384]{1,0:T(8,128)(2,1)}) %all-gather.11.cloned.1.call-update) | async-done | bytes 3932176 | tf_op jit(solution)/shard_map/all_gather | solution.py:48
  349.5 0.0 copy-done.3
  349.5 5.8 %multiply_reduce_fusion = (f32[]{:T(128)}, f32[320,384]{1,0:T(8,128)S(1)}) fusion(bf16[320,384]{1,0:T(8,128)(2,1)S(1)} %copy-done.3, bf16[5120,384]{1,0:T(8,128)(2,1)} %all-gather.11.cloned.1.call-done, bf16[5120,608]{1,0:T(8,128)(2,1)} %reshape.20), kind=kOutput, calls=%fused_computation.25 | convolution fusion | flops 1258659840 | bytes 8601604 | tf_op jit(solution)/shard_map/dot_general | solution.py:52
  355.3 95.2 %psum.7 = f32[]{:T(128)} all-reduce(f32[]{:T(128)} %get-tuple-element.4), channel_id=1, replica_groups=mesh['dp'=32,'fsdp'=16] {'dp','fsdp'}, use_global_device_ids=true, to_apply=%region_2.0 | all-reduce | flops 1 | bytes 8 | tf_op jit(solution)/shard_map/psum | solution.py:53
  451.2 0.0 copy-done.2
  451.2 1.0 fusion.11
  452.2 0.0 all-gather.13.cloned.1.call-update
  452.2 73.9 %all-gather.13.cloned.1.call-done = bf16[5120,384]{1,0:T(8,128)(2,1)} async-done(((bf16[320,384]{1,0:T(8,128)(2,1)}), bf16[5120,384]{1,0:T(8,128)(2,1)}) %all-gather.13.cloned.1.call-update) | async-done | bytes 3932176 | tf_op jit(solution)/shard_map/all_gather | solution.py:48
  526.1 0.0 copy-done.1
  526.1 0.0 copy-done.4
  526.1 7.0 %multiply_subtract_fusion = (f32[288,384]{1,0:T(8,128)}, f32[288,384]{1,0:T(8,128)}) fusion(f32[288,384]{1,0:T(8,128)S(1)} %copy-done.1, bf16[5120,384]{1,0:T(8,128)(2,1)} %all-gather.13.cloned.1.call-done, bf16[5120,608]{1,0:T(8,128)(2,1)} %reshape.20, f32[288,384]{1,0:T(8,128)S(1)} %copy-done.4), kind=kOutput, calls=%fused_computation.26 | convolution fusion | flops 1132904448 | bytes 9633792 | tf_op jit(solution)/shard_map/dot_general | solution.py:56
  (1 shorter events, 0.0 us)
Async XLA Ops:
  7.2 84.8 %all-gather.15.cloned.1.call-start = ((), (), s32[]{:S(2)}) async-start(), calls=%async_computation.4 | async-start | bytes 2506752 | tf_op jit(solution)/shard_map/all_gather | solution.py:35
  7.2 6.1 %copy-start = (f32[288,384]{1,0:T(8,128)S(1)}, f32[288,384]{1,0:T(8,128)}, u32[]{:S(2)}) copy-start(f32[288,384]{1,0:T(8,128)} %param.8) | copy-start | bytes 1327108
  13.2 156.5 %all-gather.9.cloned.1.call-start = ((), (), s32[]{:S(2)}) async-start(), calls=%async_computation.1 | async-start | bytes 3760128 | tf_op jit(solution)/shard_map/all_gather | solution.py:33
  14.0 256.4 %all-gather.7.cloned.1.call-start = ((), (), s32[]{:S(2)}) async-start(), calls=%async_computation | async-start | bytes 6758400 | tf_op jit(solution)/shard_map/all_gather | solution.py:40
  99.2 250.3 %all-gather.11.cloned.1.call-start = ((), (), s32[]{:S(2)}) async-start(), calls=%async_computation.2 | async-start | bytes 4177920 | tf_op jit(solution)/shard_map/all_gather | solution.py:48
  174.3 351.8 %all-gather.13.cloned.1.call-start = ((), (), s32[]{:S(2)}) async-start(), calls=%async_computation.3 | async-start | bytes 4177920 | tf_op jit(solution)/shard_map/all_gather | solution.py:48
  292.4 57.0 %copy-start.3 = (bf16[320,384]{1,0:T(8,128)(2,1)S(1)}, bf16[320,384]{1,0:T(8,128)(2,1)}, u32[]{:S(2)}) copy-start(bf16[320,384]{1,0:T(8,128)(2,1)} %get-tuple-element.2) | copy-start | bytes 737284
  306.1 145.2 %copy-start.2 = (bf16[320,384]{1,0:T(8,128)(2,1)S(1)}, bf16[320,384]{1,0:T(8,128)(2,1)}, u32[]{:S(2)}) copy-start(bf16[320,384]{1,0:T(8,128)(2,1)} %param.6) | copy-start | bytes 737284
  306.1 220.0 %copy-start.1 = (f32[288,384]{1,0:T(8,128)S(1)}, f32[288,384]{1,0:T(8,128)}, u32[]{:S(2)}) copy-start(f32[288,384]{1,0:T(8,128)} %param.8) | copy-start | bytes 1327108
  306.1 220.0 %copy-start.4 = (f32[288,384]{1,0:T(8,128)S(1)}, f32[288,384]{1,0:T(8,128)}, u32[]{:S(2)}) copy-start(f32[288,384]{1,0:T(8,128)} %param.9) | copy-start | bytes 1327108
Sparse Core Ops, SparseCore 0:
  13.3 78.5 all-gather.14
  94.6 75.0 all-gather.8
  173.6 96.6 all-gather.6
  272.9 76.5 all-gather.10
  452.3 73.7 all-gather.12
where the time goes:
time: 541 us; the launch traced here: 540 us
  waiting for transfers between devices  362 us (67%)
  blocking collectives  95.2 us (18%)
  local copies, waits for them, and re-layouts  40.2 us (7%)
  matrix products  20 us (4%)
  between operations  14.6 us (3%)
  other arithmetic  7.69 us (1%)
    all_gather x2, waiting for transfers between devices, gathered(): return (dpre, lax.all_gather(dpre, 'fsdp', axis=0, tiled=True))  117 us
    all_gather x1, waiting for transfers between devices, local(): lax.all_gather(jnp.concatenate([gram, columns], axis=1), 'dp', axis=0, ti...  96.1 us
    psum x1, blocking collectives, local(): lax.psum(jnp.sum(dpre.astype(jnp.float32) * shift), ('dp', 'fsdp'))  95.2 us
    all_gather x1, waiting for transfers between devices, local(): some = lax.all_gather(mine, 'fsdp', axis=0, tiled=True)  77.9 us
    all_gather x1, waiting for transfers between devices, local(): lax.all_gather(master.astype(jnp.bfloat16), 'fsdp', axis=0, tiled=True)  70.5 us
    reshape x1, local copies, waits for them, and re-layouts, local(): both.transpose(1, 0, 2, 3)  13.6 us
    reshape x1, local copies, waits for them, and re-layouts, local(): both = both.reshape(n_copy, n_shard, share, own_tokens + own_rows)  12.8 us
  transfers between devices with their start and end apart: 5, of which 5 were waited for; matrix products, arithmetic and copies ran while one was open for 9% of the time, Pallas kernels for 0%

commit v1 on v0

--- a/solution.py
+++ b/solution.py
@@ -37,7 +37,12 @@
         jnp.bfloat16
     )
     columns = lax.dynamic_slice_in_dim(some, lax.axis_index("fsdp") * own_rows, own_rows, 1)
-    both = lax.all_gather(jnp.concatenate([gram, columns], axis=1), "dp", axis=0, tiled=True)
+    both = jnp.concatenate(
+        lax.all_to_all(
+            jnp.stack([jnp.concatenate([gram, columns], axis=1)] * lax.axis_size("dp")), "dp", 0, 0
+        ),
+        axis=0,
+    )
     both = both.reshape(n_copy, n_shard, share, own_tokens + own_rows)
     both = both.transpose(1, 0, 2, 3).reshape(n_shard * own_tokens, own_tokens + own_rows)
     gram_all = both[:, :own_tokens]

time: 541 us -> 498 us (0.921)
  waiting for transfers between devices: 362 us -> 299 us
  blocking collectives: 95.2 us -> 106 us
  starting transfers between devices: 0.21 us -> 10.9 us
    all_gather x1 -> x0, waiting for transfers between devices: 96.1 us -> none  [local(): lax.all_gather(jnp.concatenate([gram, columns], axis=1), 'dp', axis=0, ti...]
    all_to_all x0 -> x1, waiting for transfers between devices: none -> 76 us  [local(): lax.all_to_all(jnp.stack([jnp.concatenate([gram, columns], axis=1)] * lax...]
    all_gather x2, waiting for transfers between devices: 117 us -> 74.7 us  [gathered(): return (dpre, lax.all_gather(dpre, 'fsdp', axis=0, tiled=True))]
    reshape x1 -> x0, local copies, waits for them, and re-layouts: 12.8 us -> none  [local(): both = both.reshape(n_copy, n_shard, share, own_tokens + own_rows)]
    psum x1, blocking collectives: 95.2 us -> 106 us  [local(): lax.psum(jnp.sum(dpre.astype(jnp.float32) * shift), ('dp', 'fsdp'))]
    all_to_all x0 -> x1, starting transfers between devices: none -> 10.6 us  [local(): lax.all_to_all(jnp.stack([jnp.concatenate([gram, columns], axis=1)] * lax...]
    all_to_all x0 -> x1, local copies, waits for them, and re-layouts: none -> 7.87 us  [local(): lax.all_to_all(jnp.stack([jnp.concatenate([gram, columns], axis=1)] * lax...]
  transfers between devices with their start and end apart: 5 -> 5, of which waited for: 5 -> 4; matrix products, arithmetic and copies ran while one was open for 9% -> 9% of each run, Pallas kernels for 0% -> 0%
where the time goes in v1:
time: 498 us; the launch traced here: 497 us
  waiting for transfers between devices  299 us (60%)
  blocking collectives  106 us (21%)
  local copies, waits for them, and re-layouts  39.4 us (8%)
  matrix products  20.1 us (4%)
  between operations  14.6 us (3%)
  starting transfers between devices  10.9 us (2%)
  other arithmetic  7.01 us (1%)
    psum x1, blocking collectives, local(): lax.psum(jnp.sum(dpre.astype(jnp.float32) * shift), ('dp', 'fsdp'))  106 us
    all_gather x1, waiting for transfers between devices, local(): some = lax.all_gather(mine, 'fsdp', axis=0, tiled=True)  78 us
    all_to_all x1, waiting for transfers between devices, local(): lax.all_to_all(jnp.stack([jnp.concatenate([gram, columns], axis=1)] * lax...  76 us
    all_gather x2, waiting for transfers between devices, gathered(): return (dpre, lax.all_gather(dpre, 'fsdp', axis=0, tiled=True))  74.7 us
    all_gather x1, waiting for transfers between devices, local(): lax.all_gather(master.astype(jnp.bfloat16), 'fsdp', axis=0, tiled=True)  70.2 us
    reshape x1, local copies, waits for them, and re-layouts, local(): both.transpose(1, 0, 2, 3)  13.6 us
    all_to_all x1, starting transfers between devices, local(): lax.all_to_all(jnp.stack([jnp.concatenate([gram, columns], axis=1)] * lax...  10.6 us
    transpose x1, local copies, waits for them, and re-layouts, local(): both.transpose(1, 0, 2, 3)  10.2 us
  transfers between devices with their start and end apart: 5, of which 4 were waited for; matrix products, arithmetic and copies ran while one was open for 9% of the time, Pallas kernels for 0%

profile of v1, /device:TPU:4, one launch (start us, length us, event | category | flops | bytes accessed | tf_op | source)
XLA Modules:
  0.0 497.2 jit_solution(4451255214298321469)
XLA Ops:
  7.2 0.0 all-gather.12.cloned.1.call-start
  7.2 0.0 copy-start
  7.2 2.6 fusion
  9.8 2.7 fusion.2
  12.5 0.7 dynamic-slice_bitcast_fusion
  13.2 0.0 all-gather.12.cloned.1.call-update
  13.2 0.0 all-gather.6.cloned.1.call-start
  13.3 0.0 copy-done
  13.3 0.7 convert_element_type.28
  14.0 0.0 all-gather.6.cloned.1.call-update
  14.0 78.0 %all-gather.12.cloned.1.call-done = bf16[16,10,4608]{2,1,0:T(8,128)(2,1)} async-done(((bf16[1,10,4608]{2,1,0:T(8,128)(2,1)}), bf16[16,10,4608]{2,1,0:T(8,128)(2,1)}) %all-gather.12.cloned.1.call-update) | async-done | bytes 1474576 | tf_op jit(solution)/shard_map/all_gather | solution.py:35
  92.0 2.8 reshape.20
  94.7 1.0 constant_dynamic-slice_fusion
  95.7 2.6 convolution_convert_fusion
  98.4 0.1 pad_maximum_fusion
  98.5 3.2 stack.2
  101.7 10.6 %all-to-all-start = ((bf16[32,160,608]{2,1,0:T(8,128)(2,1)}), bf16[32,160,608]{2,1,0:T(8,128)(2,1)}, u32[]{:S(2)}, u32[]{:S(2)}) async-start(bf16[32,160,608]{2,1,0:T(8,128)(2,1)} %stack.2), calls=%async_computation | async-start | bytes 13107200 | tf_op jit(solution)/shard_map/all_to_all | solution.py:41
  112.3 0.0 all-gather.8.cloned.1.call-start
  112.3 70.2 %all-gather.6.cloned.1.call-done = bf16[4608,384]{1,0:T(8,128)(2,1)} async-done(((bf16[288,384]{1,0:T(8,128)(2,1)}), bf16[4608,384]{1,0:T(8,128)(2,1)}) %all-gather.6.cloned.1.call-update) | async-done | bytes 3538960 | tf_op jit(solution)/shard_map/all_gather | solution.py:33
  182.5 4.5 fusion.10
  187.1 0.0 all-gather.8.cloned.1.call-update
  187.1 0.2 all-gather.10.cloned.1.call-start
  187.3 76.0 %all-to-all-done = bf16[32,160,608]{2,1,0:T(8,128)(2,1)} async-done(((bf16[32,160,608]{2,1,0:T(8,128)(2,1)}), bf16[32,160,608]{2,1,0:T(8,128)(2,1)}, u32[]{:S(2)}, u32[]{:S(2)}) %all-to-all-start) | async-done | bytes 6225952 | tf_op jit(solution)/shard_map/all_to_all | solution.py:41
  263.3 7.9 %copy.8 = bf16[32,160,608]{2,0,1:T(8,128)(2,1)} copy(bf16[32,160,608]{2,1,0:T(8,128)(2,1)} %all-to-all-done) | data formatting | bytes 12451840 | tf_op jit(solution)/shard_map/all_to_all | solution.py:41
  271.2 10.2 %copy.9 = bf16[16,32,10,608]{3,2,1,0:T(8,128)(2,1)} copy(bf16[16,32,10,608]{3,1,2,0:T(8,128)(2,1)} %bitcast.11) | data formatting | bytes 12451840 | tf_op jit(solution)/shard_map/transpose | solution.py:47
  281.4 0.0 copy-start.3
  281.4 13.6 %reshape.18 = bf16[5120,608]{1,0:T(8,128)(2,1)} reshape(bf16[16,32,10,608]{3,2,1,0:T(8,128)(2,1)} %copy.9) | data formatting | bytes 12451840 | tf_op jit(solution)/shard_map/reshape | solution.py:47
  295.0 0.0 copy-start.2
  295.0 0.0 copy-start.1
  295.0 0.0 copy-start.4
  295.0 0.0 all-gather.8.cloned.1.call-done
  295.1 0.0 copy-done.3
  295.1 5.9 %multiply_reduce_fusion = (f32[]{:T(128)}, f32[320,384]{1,0:T(8,128)S(1)}) fusion(bf16[320,384]{1,0:T(8,128)(2,1)S(1)} %copy-done.3, bf16[5120,384]{1,0:T(8,128)(2,1)} %all-gather.8.cloned.1.call-done, bf16[5120,608]{1,0:T(8,128)(2,1)} %reshape.18), kind=kOutput, calls=%fused_computation.25 | convolution fusion | flops 1258659840 | bytes 8601604 | tf_op jit(solution)/shard_map/dot_general | solution.py:57
  301.0 106.3 %psum.7 = f32[]{:T(128)} all-reduce(f32[]{:T(128)} %get-tuple-element.4), channel_id=1, replica_groups=mesh['dp'=32,'fsdp'=16] {'dp','fsdp'}, use_global_device_ids=true, to_apply=%region_2.0 | all-reduce | flops 1 | bytes 8 | tf_op jit(solution)/shard_map/psum | solution.py:58
  408.0 0.0 copy-done.2
  408.0 1.0 fusion.11
  409.0 0.0 all-gather.10.cloned.1.call-update
  409.0 74.7 %all-gather.10.cloned.1.call-done = bf16[5120,384]{1,0:T(8,128)(2,1)} async-done(((bf16[320,384]{1,0:T(8,128)(2,1)}), bf16[5120,384]{1,0:T(8,128)(2,1)}) %all-gather.10.cloned.1.call-update) | async-done | bytes 3932176 | tf_op jit(solution)/shard_map/all_gather | solution.py:53
  483.7 0.0 copy-done.1
  483.7 0.0 copy-done.4
  483.7 7.0 %multiply_subtract_fusion = (f32[288,384]{1,0:T(8,128)}, f32[288,384]{1,0:T(8,128)}) fusion(f32[288,384]{1,0:T(8,128)S(1)} %copy-done.1, bf16[5120,384]{1,0:T(8,128)(2,1)} %all-gather.10.cloned.1.call-done, bf16[5120,608]{1,0:T(8,128)(2,1)} %reshape.18, f32[288,384]{1,0:T(8,128)S(1)} %copy-done.4), kind=kOutput, calls=%fused_computation.26 | convolution fusion | flops 1132904448 | bytes 9633792 | tf_op jit(solution)/shard_map/dot_general | solution.py:61
  (1 shorter events, 0.0 us)
Async XLA Ops:
  7.2 84.8 %all-gather.12.cloned.1.call-start = ((), (), s32[]{:S(2)}) async-start(), calls=%async_computation.4 | async-start | bytes 2506752 | tf_op jit(solution)/shard_map/all_gather | solution.py:35
  7.2 6.1 %copy-start = (f32[288,384]{1,0:T(8,128)S(1)}, f32[288,384]{1,0:T(8,128)}, u32[]{:S(2)}) copy-start(f32[288,384]{1,0:T(8,128)} %param.8) | copy-start | bytes 1327108
  13.2 169.3 %all-gather.6.cloned.1.call-start = ((), (), s32[]{:S(2)}) async-start(), calls=%async_computation.1 | async-start | bytes 3760128 | tf_op jit(solution)/shard_map/all_gather | solution.py:33
  101.7 161.6 %all-to-all-start = ((bf16[32,160,608]{2,1,0:T(8,128)(2,1)}), bf16[32,160,608]{2,1,0:T(8,128)(2,1)}, u32[]{:S(2)}, u32[]{:S(2)}) async-start(bf16[32,160,608]{2,1,0:T(8,128)(2,1)} %stack.2), calls=%async_computation | async-start | bytes 13107200 | tf_op jit(solution)/shard_map/all_to_all | solution.py:41
  112.3 182.8 %all-gather.8.cloned.1.call-start = ((), (), s32[]{:S(2)}) async-start(), calls=%async_computation.2 | async-start | bytes 4177920 | tf_op jit(solution)/shard_map/all_gather | solution.py:53
  187.1 296.6 %all-gather.10.cloned.1.call-start = ((), (), s32[]{:S(2)}) async-start(), calls=%async_computation.3 | async-start | bytes 4177920 | tf_op jit(solution)/shard_map/all_gather | solution.py:53
  281.4 13.6 %copy-start.3 = (bf16[320,384]{1,0:T(8,128)(2,1)S(1)}, bf16[320,384]{1,0:T(8,128)(2,1)}, u32[]{:S(2)}) copy-start(bf16[320,384]{1,0:T(8,128)(2,1)} %get-tuple-element.2) | copy-start | bytes 737284
  295.0 113.0 %copy-start.2 = (bf16[320,384]{1,0:T(8,128)(2,1)S(1)}, bf16[320,384]{1,0:T(8,128)(2,1)}, u32[]{:S(2)}) copy-start(bf16[320,384]{1,0:T(8,128)(2,1)} %param.6) | copy-start | bytes 737284
  295.0 188.6 %copy-start.1 = (f32[288,384]{1,0:T(8,128)S(1)}, f32[288,384]{1,0:T(8,128)}, u32[]{:S(2)}) copy-start(f32[288,384]{1,0:T(8,128)} %param.8) | copy-start | bytes 1327108
  295.0 188.6 %copy-start.4 = (f32[288,384]{1,0:T(8,128)S(1)}, f32[288,384]{1,0:T(8,128)}, u32[]{:S(2)}) copy-start(f32[288,384]{1,0:T(8,128)} %param.9) | copy-start | bytes 1327108
Sparse Core Ops, SparseCore 0:
  13.3 78.5 all-gather.11
  94.6 87.8 all-gather.5
  187.2 91.4 all-gather.7
  409.1 74.4 all-gather.9
